TPU v7x, 32 devices: a whole 2x2x4 slice. The times are simulated.
32 devices in a mesh: row: 4 (over z), col: 4 (over x, core), chol: 2 (over y).
Axes of the slice: x: 2, y: 2, z: 4, core: 2. Of those that a mesh axis runs over, the one named last changes fastest.
Arguments:
- left_vectors: bfloat16 [64, 4608, 1536], P(None, ('col', 'chol'), 'row'), may hold values from -0.75 to 0.75
- right_vectors: bfloat16 [16, 4608, 1536], P(None, ('col', 'chol'), 'row'), may hold values from -0.0234375 to 0.0234375
- amplitudes: bfloat16 [8, 16, 64], replicated, may hold values from -6 to 6
Outputs:
- ladder: float32 [8, 1536, 1536], P('chol', 'row', 'col')
All inputs are finite; a program needn't handle non-finite values.
Results may differ from a plain program's by a relative error of at most 0.0029.
Values may be sent and summed in bfloat16 or wider, within the bound.
No kernel may reach another device: no remote copies, remote signals or barrier semaphores. Data moves between devices by JAX's collectives and lax.ppermute only.
A program may use at most 256 MiB of HBM per device.

v0:
```python
import jax
import jax.numpy as jnp
from jax import lax
from jax.sharding import PartitionSpec as P


def shards(left_vectors, right_vectors, amplitudes):
    pairs, d_block, c_block = amplitudes.shape
    amp_rows = amplitudes.reshape(pairs * d_block, c_block)
    width_a = left_vectors.shape[2]
    right_full = lax.all_gather(right_vectors, "row", axis=2, tiled=True)
    columns = lax.axis_size("col")
    width_b = right_full.shape[2] // columns
    vectors = left_vectors.shape[1]
    halved = jnp.dot(
        amp_rows,
        left_vectors.reshape(c_block, vectors * width_a),
        preferred_element_type=jnp.float32,
    ).astype(jnp.bfloat16)
    halved = halved.reshape(pairs, d_block * vectors, width_a)
    panel = right_full.reshape(d_block * vectors, columns, width_b)
    ladder = jnp.einsum("ika,kcb->ciab", halved, panel, preferred_element_type=jnp.float32)
    ladder = ladder.reshape(columns * pairs, width_a, width_b)
    return lax.psum_scatter(ladder, ("col", "chol"), scatter_dimension=0, tiled=True)


def solution(mesh):
    return jax.shard_map(
        shards,
        mesh=mesh,
        in_specs=(P(None, ("col", "chol"), "row"), P(None, ("col", "chol"), "row"), P()),
        out_specs=P("chol", "row", "col"),
        check_vma=False,
    )
```

profile of v0, /device:TPU:0, one launch (start us, length us, event | category | flops | bytes accessed | tf_op | source)
XLA Modules:
  0.0 779.7 jit_solution(12643023936817732366)
XLA Ops:
  6.5 0.0 copy-start
  6.5 0.0 all-gather.2.cloned.1.call-start
  6.5 0.7 all-gather.2.cloned.1.call-update
  7.3 0.0 reduce-scatter.2.cloned.1.call-start
  7.3 40.3 %copy.11 = bf16[8,8,576,384]{3,1,2,0:T(8,128)(2,1)} copy(bf16[8,8,576,384]{3,2,1,0:T(8,128)(2,1)} %bitcast.23) | data formatting | bytes 56623104
  47.6 0.0 copy-done
  47.6 38.6 %convolution_convert_fusion = bf16[128,221184]{1,0:T(8,128)(2,1)} fusion(bf16[128,64]{1,0:T(8,128)(2,1)S(1)} %bitcast.20, bf16[64,221184]{1,0:T(8,128)(2,1)} %bitcast.21), kind=kOutput, calls=%fused_computation | convolution fusion | flops 3652190208 | bytes 84951040 | tf_op jit(solution)/shard_map/dot_general | solution.py:15
  86.2 50.1 %reshape.17 = bf16[8,9216,384]{2,1,0:T(8,128)(2,1)} reshape(bf16[128,221184]{1,0:T(8,128)(2,1)} %convolution_convert_fusion) | data formatting | bytes 113246208 | tf_op jit(solution)/shard_map/reshape | solution.py:20
  136.3 351.5 %all-gather.2.cloned.1.call-done = bf16[16,576,1536]{2,1,0:T(8,128)(2,1)} async-done(((bf16[16,576,384]{2,1,0:T(8,128)(2,1)}), bf16[16,576,1536]{2,1,0:T(8,128)(2,1)}) %all-gather.2.cloned.1.call-update) | async-done | bytes 28311568 | tf_op jit(solution)/shard_map/all_gather | solution.py:11
  487.8 47.2 %reshape.18 = bf16[9216,4,384]{2,1,0:T(4,128)(2,1)} reshape(bf16[16,576,1536]{2,1,0:T(8,128)(2,1)} %all-gather.2.cloned.1.call-done) | data formatting | bytes 56623104 | tf_op jit(solution)/shard_map/reshape | solution.py:21
  535.0 0.0 copy-start.1
  535.0 100.5 %fusion.4 = f32[4,8,384,384]{3,2,0,1:T(8,128)} fusion(bf16[9216,4,384]{2,1,0:T(4,128)(2,1)} %reshape.18, bf16[8,9216,384]{2,1,0:T(8,128)(2,1)} %reshape.17), kind=kOutput, calls=%fused_computation.5 | convolution fusion | flops 86973087744 | bytes 103809024 | tf_op jit(solution)/shard_map/ika,kcb->ciab/dot_general | solution.py:22
  635.5 12.6 %copy.7 = f32[4,8,384,384]{3,2,1,0:T(8,128)} copy(f32[4,8,384,384]{3,2,0,1:T(8,128)} %fusion.4) | data formatting | bytes 37748736 | tf_op jit(solution)/shard_map/ika,kcb->ciab/transpose | solution.py:22
  648.1 0.0 reduce-scatter.2.cloned.1.call-update
  648.1 124.8 %reduce-scatter.2.cloned.1.call-done = f32[4,384,384]{2,1,0:T(8,128)} async-done(((f32[32,384,384]{2,1,0:T(8,128)}), f32[4,384,384]{2,1,0:T(8,128)}) %reduce-scatter.2.cloned.1.call-update) | async-done | bytes 2359312 | tf_op jit(solution)/shard_map/reduce_scatter | solution.py:24
  772.9 0.0 copy-done.1
Async XLA Ops:
  6.5 41.1 %copy-start = (bf16[8,16,64]{2,1,0:T(8,128)(2,1)S(1)}, bf16[8,16,64]{2,1,0:T(8,128)(2,1)}, u32[]{:S(2)}) copy-start(bf16[8,16,64]{2,1,0:T(8,128)(2,1)} %param.5) | copy-start | bytes 49156
  6.5 481.3 %all-gather.2.cloned.1.call-start = ((), (), s32[]{:S(2)}) async-start(), calls=%async_computation.1 | async-start | bytes 35389440 | tf_op jit(solution)/shard_map/all_gather | solution.py:11
  7.3 765.6 %reduce-scatter.2.cloned.1.call-start = ((), (), s32[]{:S(2)}) async-start(), calls=%async_computation.2 | async-start | bytes 21233664 | tf_op jit(solution)/shard_map/reduce_scatter | solution.py:24
  535.0 237.9 %copy-start.1 = (bf16[8,16,64]{2,1,0:T(8,128)(2,1)S(1)}, bf16[8,16,64]{2,1,0:T(8,128)(2,1)}, u32[]{:S(2)}) copy-start(bf16[8,16,64]{2,1,0:T(8,128)(2,1)} %param.5) | copy-start | bytes 49156
Sparse Core Ops, SparseCore 0:
  8.9 478.8 all-gather.1
  648.3 124.6 reduce-scatter.1
where the time goes:
time: 782 us; the launch traced here: 780 us
  waiting for transfers between devices  477 us (61%)
  local copies, waits for them, and re-layouts  150 us (19%)
  matrix products  139 us (18%)
  between operations  13.4 us (2%)
    all_gather x1, waiting for transfers between devices, shards(): right_full = lax.all_gather(right_vectors, 'row', axis=2, tiled=True)  352 us
    reduce_scatter x1, waiting for transfers between devices, shards(): lax.psum_scatter(ladder, ('col', 'chol'), scatter_dimension=0, tiled=True)  125 us
    dot_general x1, matrix products, shards(): jnp.einsum('ika,kcb->ciab', halved, panel, preferred_element_type=jnp.flo...  101 us
    reshape x1, local copies, waits for them, and re-layouts, shards(): halved = halved.reshape(pairs, d_block * vectors, width_a)  50.1 us
    reshape x1, local copies, waits for them, and re-layouts, shards(): panel = right_full.reshape(d_block * vectors, columns, width_b)  47.2 us
    unnamed x5, local copies, waits for them, and re-layouts  40.3 us
    dot_general x1, matrix products, shards(): jnp.dot(amp_rows, left_vectors.reshape(c_block, vectors * width_a), prefe...  38.6 us
  transfers between devices with their start and end apart: 2, of which 2 were waited for; matrix products, arithmetic and copies ran while one was open for 17% of the time, Pallas kernels for 0%

commit v1 on v0

--- a/solution.py
+++ b/solution.py
@@ -8,7 +8,10 @@
     pairs, d_block, c_block = amplitudes.shape
     amp_rows = amplitudes.reshape(pairs * d_block, c_block)
     width_a = left_vectors.shape[2]
-    right_full = lax.all_gather(right_vectors, "row", axis=2, tiled=True)
+    n_dev = lax.axis_size("row")
+    pieces = jnp.stack([right_vectors for _ in range(n_dev)])
+    pieces = lax.all_to_all(pieces, "row", split_axis=0, concat_axis=0)
+    right_full = jnp.concatenate(pieces, axis=2)
     columns = lax.axis_size("col")
     width_b = right_full.shape[2] // columns
     vectors = left_vectors.shape[1]

time: 782 us -> 887 us (1.13)
  waiting for transfers between devices: 477 us -> 609 us
  local copies, waits for them, and re-layouts: 150 us -> 117 us
  starting transfers between devices: 0.04 us -> 8.92 us
    all_to_all x0 -> x1, waiting for transfers between devices: none -> 483 us  [shards(): pieces = lax.all_to_all(pieces, 'row', split_axis=0, concat_axis=0)]
    all_gather x1 -> x0, waiting for transfers between devices: 352 us -> none  [shards(): right_full = lax.all_gather(right_vectors, 'row', axis=2, tiled=True)]
    reshape x1 -> x0, local copies, waits for them, and re-layouts: 47.2 us -> none  [shards(): panel = right_full.reshape(d_block * vectors, columns, width_b)]
    another operation x0 -> x1, local copies, waits for them, and re-layouts: none -> 14.4 us  [shards(): pieces = jnp.stack([right_vectors for _ in range(n_dev)])]
    all_to_all x0 -> x1, starting transfers between devices: none -> 8.87 us  [shards(): pieces = lax.all_to_all(pieces, 'row', split_axis=0, concat_axis=0)]
  transfers between devices with their start and end apart: 2 -> 2, of which waited for: 2 -> 2; matrix products, arithmetic and copies ran while one was open for 17% -> 15% of each run, Pallas kernels for 0% -> 0%
where the time goes in v1:
time: 887 us; the launch traced here: 886 us
  waiting for transfers between devices  609 us (69%)
  matrix products  137 us (15%)
  local copies, waits for them, and re-layouts  117 us (13%)
  between operations  13.4 us (2%)
  starting transfers between devices  8.92 us (1%)
    all_to_all x1, waiting for transfers between devices, shards(): pieces = lax.all_to_all(pieces, 'row', split_axis=0, concat_axis=0)  483 us
    reduce_scatter x1, waiting for transfers between devices, shards(): lax.psum_scatter(ladder, ('col', 'chol'), scatter_dimension=0, tiled=True)  126 us
    dot_general x1, matrix products, shards(): jnp.einsum('ika,kcb->ciab', halved, panel, preferred_element_type=jnp.flo...  98.8 us
    reshape x1, local copies, waits for them, and re-layouts, shards(): halved = halved.reshape(pairs, d_block * vectors, width_a)  50.1 us
    unnamed x5, local copies, waits for them, and re-layouts  40.3 us
    dot_general x1, matrix products, shards(): jnp.dot(amp_rows, left_vectors.reshape(c_block, vectors * width_a), prefe...  38.3 us
  transfers between devices with their start and end apart: 2, of which 2 were waited for; matrix products, arithmetic and copies ran while one was open for 15% of the time, Pallas kernels for 0%

profile of v1, /device:TPU:0, one launch (start us, length us, event | category | flops | bytes accessed | tf_op | source)
XLA Modules:
  0.0 885.6 jit_solution(5520400525623550320)
XLA Ops:
  6.5 0.0 copy-start
  6.5 14.4 %stack.2 = bf16[4,16,576,384]{3,2,1,0:T(8,128)(2,1)} broadcast(bf16[16,576,384]{2,1,0:T(8,128)(2,1)} %param.4), dimensions={1,2,3} | broadcast | bytes 35389440 | tf_op jit(solution)/shard_map/stack | solution.py:12
  21.0 8.9 %all-to-all-start = ((bf16[4,16,576,384]{3,2,1,0:T(8,128)(2,1)}), bf16[4,16,576,384]{3,2,1,0:T(8,128)(2,1)}, u32[]{:S(2)}, u32[]{:S(2)}) async-start(bf16[4,16,576,384]{3,2,1,0:T(8,128)(2,1)} %stack.2), calls=%async_computation | async-start | bytes 56623104 | tf_op jit(solution)/shard_map/all_to_all | solution.py:13
  29.9 0.0 reduce-scatter.2.cloned.1.call-start
  29.9 40.3 %copy.10 = bf16[8,8,576,384]{3,1,2,0:T(8,128)(2,1)} copy(bf16[8,8,576,384]{3,2,1,0:T(8,128)(2,1)} %bitcast.24) | data formatting | bytes 56623104
  70.2 0.0 copy-done
  70.2 38.3 %convolution_convert_fusion = bf16[128,221184]{1,0:T(8,128)(2,1)} fusion(bf16[128,64]{1,0:T(8,128)(2,1)S(1)} %bitcast.21, bf16[64,221184]{1,0:T(8,128)(2,1)} %bitcast.22), kind=kOutput, calls=%fused_computation | convolution fusion | flops 3652190208 | bytes 84951040 | tf_op jit(solution)/shard_map/dot_general | solution.py:18
  108.5 50.1 %reshape.19 = bf16[8,9216,384]{2,1,0:T(8,128)(2,1)} reshape(bf16[128,221184]{1,0:T(8,128)(2,1)} %convolution_convert_fusion) | data formatting | bytes 113246208 | tf_op jit(solution)/shard_map/reshape | solution.py:23
  158.6 483.0 %all-to-all-done = bf16[4,16,576,384]{3,2,1,0:T(8,128)(2,1)} async-done(((bf16[4,16,576,384]{3,2,1,0:T(8,128)(2,1)}), bf16[4,16,576,384]{3,2,1,0:T(8,128)(2,1)}, u32[]{:S(2)}, u32[]{:S(2)}) %all-to-all-start) | async-done | bytes 28311584 | tf_op jit(solution)/shard_map/all_to_all | solution.py:13
  641.6 0.0 copy-start.1
  641.6 98.8 %fusion.2 = f32[4,8,384,384]{3,2,0,1:T(8,128)} fusion(bf16[9216,4,384,1]{2,0,1,3:T(8,128)(2,1)} %bitcast.4, bf16[8,9216,384]{2,1,0:T(8,128)(2,1)} %reshape.19), kind=kOutput, calls=%fused_computation.3 | convolution fusion | flops 86973087744 | bytes 103809024 | tf_op jit(solution)/shard_map/ika,kcb->ciab/dot_general | solution.py:25
  740.4 12.6 %copy.6 = f32[4,8,384,384]{3,2,1,0:T(8,128)} copy(f32[4,8,384,384]{3,2,0,1:T(8,128)} %fusion.2) | data formatting | bytes 37748736 | tf_op jit(solution)/shard_map/ika,kcb->ciab/transpose | solution.py:25
  753.0 0.0 reduce-scatter.2.cloned.1.call-update
  753.0 125.8 %reduce-scatter.2.cloned.1.call-done = f32[4,384,384]{2,1,0:T(8,128)} async-done(((f32[32,384,384]{2,1,0:T(8,128)}), f32[4,384,384]{2,1,0:T(8,128)}) %reduce-scatter.2.cloned.1.call-update) | async-done | bytes 2359312 | tf_op jit(solution)/shard_map/reduce_scatter | solution.py:27
  878.8 0.0 copy-done.1
Async XLA Ops:
  6.5 63.7 %copy-start = (bf16[8,16,64]{2,1,0:T(8,128)(2,1)S(1)}, bf16[8,16,64]{2,1,0:T(8,128)(2,1)}, u32[]{:S(2)}) copy-start(bf16[8,16,64]{2,1,0:T(8,128)(2,1)} %param.5) | copy-start | bytes 49156
  21.0 620.6 %all-to-all-start = ((bf16[4,16,576,384]{3,2,1,0:T(8,128)(2,1)}), bf16[4,16,576,384]{3,2,1,0:T(8,128)(2,1)}, u32[]{:S(2)}, u32[]{:S(2)}) async-start(bf16[4,16,576,384]{3,2,1,0:T(8,128)(2,1)} %stack.2), calls=%async_computation | async-start | bytes 56623104 | tf_op jit(solution)/shard_map/all_to_all | solution.py:13
  29.9 848.9 %reduce-scatter.2.cloned.1.call-start = ((), (), s32[]{:S(2)}) async-start(), calls=%async_computation.2 | async-start | bytes 21233664 | tf_op jit(solution)/shard_map/reduce_scatter | solution.py:27
  641.6 237.2 %copy-start.1 = (bf16[8,16,64]{2,1,0:T(8,128)(2,1)S(1)}, bf16[8,16,64]{2,1,0:T(8,128)(2,1)}, u32[]{:S(2)}) copy-start(bf16[8,16,64]{2,1,0:T(8,128)(2,1)} %param.5) | copy-start | bytes 49156
Sparse Core Ops, SparseCore 0:
  753.2 125.5 reduce-scatter.1
